TPU v7x, 256 devices: a whole 4x4x8 slice. The times are simulated.
256 devices in a mesh: col: 64 (over z, x, core), row: 4 (over y).
Axes of the slice: x: 4, y: 4, z: 8, core: 2. Of those that a mesh axis runs over, the one named last changes fastest.
Arguments:
- matrix: float32 [16, 512, 1, 8192], P(None, 'row', None, 'col'), may hold values from -1 to 5, as said below
- inverse_factors: float32 [2, 512, 512], replicated, may hold values from -1 to 1, as said below
Outputs:
- factored: float32 [16, 512, 1, 8192], P(None, 'row', None, 'col')
Inputs may be any that keep to these rules, and one draw needn't show every extreme that they name: matrix holds a symmetric matrix. Each inverse_factors[k] is lower triangular with a positive diagonal; it is given independently of matrix.
All inputs are finite; a program needn't handle non-finite values.
Results may differ from a plain program's by a relative error of at most 0.0001.
Values sent between devices are 32-bit elements; how exact they have to be, the bound alone decides.
No kernel may reach another device: no remote copies, remote signals or barrier semaphores. Data moves between devices by JAX's collectives and lax.ppermute only.
A program may use at most 64 MiB of HBM per device.

v0:
```python
import jax
import jax.numpy as jnp
from jax import lax
from jax.sharding import PartitionSpec as P


def broadcast(x, axis, root):
    mine = lax.axis_index(axis) == root
    return lax.psum(jnp.where(mine, x, jnp.zeros_like(x)), axis)


def exact_dot(left_side, right_side):
    return jnp.dot(
        left_side, right_side, precision=lax.Precision.HIGHEST, preferred_element_type=jnp.float32
    )


def shards(matrix, inverse_factors):
    col_count = lax.axis_size("col")
    row_count = lax.axis_size("row")
    col_index = lax.axis_index("col")
    row_index = lax.axis_index("row")
    row_blocks, block_cols, cycles, _ = matrix.shape
    panel_width = inverse_factors.shape[1]
    per_panel = panel_width // block_cols
    local_rows = row_blocks * block_cols
    square_view = matrix.reshape(local_rows, cycles * block_cols)
    global_rows = (
        (jnp.arange(row_blocks)[:, None] * row_count + row_index) * block_cols
        + jnp.arange(block_cols)[None, :]
    ).reshape(-1)
    take_index = (jnp.arange(cycles) * col_count + col_index) // row_count
    row_root = col_index % row_count

    def masked(factor_cols, offset):
        return jnp.where(global_rows[:, None] >= offset, factor_cols, 0.0)

    current = square_view
    for panel in range(2):
        factor = inverse_factors[panel]
        pieces = [
            broadcast(current, "col", panel * per_panel + member) for member in range(per_panel)
        ]
        factor_cols = exact_dot(jnp.concatenate(pieces, axis=1), factor.T)
        trailing = masked(factor_cols, (panel + 1) * panel_width)
        blocked = trailing.reshape(row_blocks, block_cols, panel_width)
        picked = jnp.take(blocked, take_index, axis=0).reshape(cycles * block_cols, panel_width)
        gathered = lax.all_gather(picked, "row", axis=0, tiled=True)
        column_part = lax.dynamic_slice_in_dim(
            gathered, row_root * picked.shape[0], picked.shape[0], 0
        )
        current = current - exact_dot(trailing, column_part.T)
        place_factor_cols = masked(factor_cols, panel * panel_width)
        offset_id = col_index - panel * per_panel
        inside = (offset_id >= 0) & (offset_id < per_panel)
        position = jnp.clip(offset_id, 0, per_panel - 1)
        chosen = lax.dynamic_slice_in_dim(place_factor_cols, position * block_cols, block_cols, 1)
        leading = jnp.where(inside, chosen, current)
        current = jnp.concatenate([leading, current[:, block_cols:]], axis=1)
    return current.reshape(row_blocks, block_cols, cycles, block_cols)


def solution(mesh):
    return jax.shard_map(
        shards,
        mesh=mesh,
        in_specs=(P(None, "row", None, "col"), P()),
        out_specs=P(None, "row", None, "col"),
        check_vma=False,
    )
```

profile of v0, /device:TPU:2, one launch (start us, length us, event | category | flops | bytes accessed | tf_op | source)
XLA Modules:
  0.0 504.0 jit_solution(6828557385005431134)
XLA Ops:
  6.5 0.0 all-reduce.7.cloned.1.call-start
  6.5 3.4 broadcast_select_fusion.9
  10.0 0.0 all-reduce.7.cloned.1.call-update
  10.0 0.0 all-gather.5.cloned.1.call-start
  10.1 0.1 fusion.31
  10.2 199.4 %all-reduce.7.cloned.1.call-done = (f32[2048,128]{1,0:T(8,128)}, f32[2048,128]{1,0:T(8,128)}, f32[2048,128]{1,0:T(8,128)}, f32[2048,128]{1,0:T(8,128)}) async-done(((f32[2048,128]{1,0:T(8,128)}, f32[2048,128]{1,0:T(8,128)}, f32[2048,128]{1,0:T(8,128)}, f32[2048,128]{1,0:T(8,128)}), (f32[2048,128]{1,0:T(8,128)}, f32[2048,128]{1,0:T(8,128)}, f32[2048,128]{1,0:T(8,128)}, ...) | async-done | bytes 4194320 | tf_op jit(solution)/shard_map/psum | solution.py:9
  209.6 0.0 copy-done.3
  209.6 9.9 %broadcast_select_fusion = (f32[2048,512]{1,0:T(8,128)S(1)}, f32[2048,512]{1,0:T(8,128)}) fusion(pred[2048]{0:T(1024)(128)(4,1)S(1)} %get-tuple-element.35, f32[2,512,512]{2,1,0:T(8,128)S(1)} %copy-done.3, f32[2048,128]{1,0:T(8,128)} %get-tuple-element.21, f32[2048,128]{1,0:T(8,128)} %get-tuple-element.22, f32[2048,128]{1,0:T(8,128)} %get-tuple-element.23, ...), kind=kOutput, calls=%fused_computation.20 | convolution fusion | flops 6446645248 | bytes 13633536 | tf_op jit(solution)/shard_map/dot_general | solution.py:13
  219.5 2.0 copy-done
  221.5 0.7 dynamic-slice_select_fusion.3
  222.2 0.0 all-gather.5.cloned.1.call-update
  222.2 0.0 all-reduce.5.cloned.1.call-start
  222.3 25.7 %all-gather.5.cloned.1.call-done = f32[1,512,512]{2,1,0:T(8,128)} async-done(((f32[1,128,512]{2,1,0:T(8,128)}), f32[1,512,512]{2,1,0:T(8,128)}) %all-gather.5.cloned.1.call-update) | async-done | bytes 1048592 | tf_op jit(solution)/shard_map/all_gather | solution.py:48
  248.0 0.0 copy-done.2
  248.0 8.0 %broadcast_select_fusion.5 = (f32[2048,128]{1,0:T(8,128)}, f32[2048,128]{1,0:T(8,128)}, f32[2048,128]{1,0:T(8,128)}, f32[2048,128]{1,0:T(8,128)}, f32[2048,128]{1,0:T(8,128)S(1)}) fusion(pred[]{:T(512)S(6)} %eq.26, pred[]{:T(512)S(6)} %eq.33, pred[]{:T(512)S(6)} %eq.32, pred[]{:T(512)S(6)} %eq.31, f32[2048,128]{1,0:T(8,128)S(1)} %bitcast.40, ...), kind=kOutput, calls=%fused_computation.31 | convolution fusion | flops 1612447744 | bytes 11798541 | tf_op jit(solution)/shard_map/dot_general | solution.py:13
  256.0 0.0 all-reduce.5.cloned.1.call-update
  256.0 0.2 all-gather.7.cloned.1.call-start
  256.3 195.5 %all-reduce.5.cloned.1.call-done = (f32[2048,128]{1,0:T(8,128)}, f32[2048,128]{1,0:T(8,128)}, f32[2048,128]{1,0:T(8,128)}, f32[2048,128]{1,0:T(8,128)}) async-done(((f32[2048,128]{1,0:T(8,128)}, f32[2048,128]{1,0:T(8,128)}, f32[2048,128]{1,0:T(8,128)}, f32[2048,128]{1,0:T(8,128)}), (f32[2048,128]{1,0:T(8,128)}, f32[2048,128]{1,0:T(8,128)}, f32[2048,128]{1,0:T(8,128)}, ...) | async-done | bytes 4194320 | tf_op jit(solution)/shard_map/psum | solution.py:9
  451.7 10.3 %broadcast_select_fusion.1 = (f32[2048,512]{1,0:T(8,128)S(1)}, f32[2048,512]{1,0:T(8,128)}) fusion(pred[2048]{0:T(1024)(128)(4,1)S(1)} %get-tuple-element.33, f32[2,512,512]{2,1,0:T(8,128)} %param.5, f32[2048,128]{1,0:T(8,128)} %get-tuple-element.17, f32[2048,128]{1,0:T(8,128)} %get-tuple-element.18, f32[2048,128]{1,0:T(8,128)} %get-tuple-element.19, ...), kind=kOutput, calls=%fused_computation.21 | convolution fusion | flops 6446645248 | bytes 13633536 | tf_op jit(solution)/shard_map/dot_general | solution.py:13
  462.0 2.0 copy-done.1
  464.0 0.7 dynamic-slice_select_fusion.2
  464.7 0.0 all-gather.7.cloned.1.call-update
  464.8 25.7 %all-gather.7.cloned.1.call-done = f32[1,512,512]{2,1,0:T(8,128)} async-done(((f32[1,128,512]{2,1,0:T(8,128)}), f32[1,512,512]{2,1,0:T(8,128)}) %all-gather.7.cloned.1.call-update) | async-done | bytes 1048592 | tf_op jit(solution)/shard_map/all_gather | solution.py:48
  490.5 7.0 %fusion.16 = f32[2048,128]{1,0:T(8,128)} fusion(f32[2048,128]{1,0:T(8,128)S(1)} %get-tuple-element.38, f32[2048,512]{1,0:T(8,128)} %copy-done.1, f32[2048,512]{1,0:T(8,128)} %get-tuple-element.40, s32[]{:T(128)S(6)} %select_n.137, pred[2048]{0:T(1024)(128)(4,1)S(1)} %get-tuple-element.35, pred[]{:T(512)S(6)} %and.21, ...), kind=kOutput, calls=%fused_computation.17 | convolution fusion | flops 1611399168 | bytes 7604233 | tf_op jit(solution)/shard_map/dot_general | solution.py:13
  (5 shorter events, 0.0 us)
Async XLA Ops:
  6.5 203.1 %all-reduce.7.cloned.1.call-start = ((), (), s32[]{:S(2)}) async-start(), calls=%async_computation.3 | async-start | bytes 8388608 | tf_op jit(solution)/shard_map/psum | solution.py:9
  6.5 203.1 %copy-start.3 = (f32[2,512,512]{2,1,0:T(8,128)S(1)}, f32[2,512,512]{2,1,0:T(8,128)}, u32[]{:S(2)}) copy-start(f32[2,512,512]{2,1,0:T(8,128)} %param.5) | copy-start | bytes 6291460
  10.0 238.0 %all-gather.5.cloned.1.call-start = ((), (), s32[]{:S(2)}) async-start(), calls=%async_computation | async-start | bytes 1310720 | tf_op jit(solution)/shard_map/all_gather | solution.py:48
  209.6 38.4 %copy-start.2 = (f32[16,128,1,128]{3,2,1,0:T(1,128)S(1)}, f32[16,128,1,128]{3,2,1,0:T(1,128)}, u32[]{:S(2)}) copy-start(f32[16,128,1,128]{3,2,1,0:T(1,128)} %param.4) | copy-start | bytes 3145732
  219.5 2.0 copy-start
  222.2 229.5 %all-reduce.5.cloned.1.call-start = ((), (), s32[]{:S(2)}) async-start(), calls=%async_computation.2 | async-start | bytes 8388608 | tf_op jit(solution)/shard_map/psum | solution.py:9
  256.0 234.5 %all-gather.7.cloned.1.call-start = ((), (), s32[]{:S(2)}) async-start(), calls=%async_computation.1 | async-start | bytes 1310720 | tf_op jit(solution)/shard_map/all_gather | solution.py:48
  462.0 2.0 copy-start.1
Sparse Core Ops, SparseCore 0:
  11.3 198.2 all-reduce.6
  222.3 25.5 all-gather.4
  256.1 195.5 all-reduce.4
  464.9 25.5 all-gather.6
where the time goes:
time: 504 us
  waiting for transfers between devices  446 us (88%)
  matrix products  35.2 us (7%)
  between operations  13.2 us (3%)
    psum x2, waiting for transfers between devices, broadcast(): return lax.psum(jnp.where(mine, x, jnp.zeros_like(x)), axis)  395 us
    all_gather x2, waiting for transfers between devices, shards(): gathered = lax.all_gather(picked, 'row', axis=0, tiled=True)  51.4 us
    dot_general x4, matrix products, exact_dot(): jnp.dot(left_side, right_side, precision=lax.Precision.HIGHEST, preferred...  35.2 us
  transfers between devices with their start and end apart: 4, of which 4 were waited for; matrix products, arithmetic and copies ran while one was open for 0% of the time, Pallas kernels for 0%

commit v1 on v0

--- a/solution.py
+++ b/solution.py
@@ -2,6 +2,22 @@
 import jax.numpy as jnp
 from jax import lax
 from jax.sharding import PartitionSpec as P
+
+
+def ring_gather(x, axis, dim):
+    ways, here, hop = (lax.axis_size(axis), lax.axis_index(axis), x.shape[dim])
+    lengths = [n * ways if d == dim else n for d, n in enumerate(x.shape)]
+    full = lax.dynamic_update_slice_in_dim(jnp.zeros(lengths, x.dtype), x, here * hop, axis=dim)
+    going_up = going_down = x
+    for far in range(1, ways // 2 + 1):
+        going_up = lax.ppermute(going_up, axis, [(d, (d + 1) % ways) for d in range(ways)])
+        full = lax.dynamic_update_slice_in_dim(full, going_up, (here - far) % ways * hop, axis=dim)
+        if 2 * far < ways:
+            going_down = lax.ppermute(going_down, axis, [(d, (d - 1) % ways) for d in range(ways)])
+            full = lax.dynamic_update_slice_in_dim(
+                full, going_down, (here + far) % ways * hop, axis=dim
+            )
+    return full
 
 
 def broadcast(x, axis, root):
@@ -45,7 +61,7 @@
         trailing = masked(factor_cols, (panel + 1) * panel_width)
         blocked = trailing.reshape(row_blocks, block_cols, panel_width)
         picked = jnp.take(blocked, take_index, axis=0).reshape(cycles * block_cols, panel_width)
-        gathered = lax.all_gather(picked, "row", axis=0, tiled=True)
+        gathered = ring_gather(picked, "row", 0)
         column_part = lax.dynamic_slice_in_dim(
             gathered, row_root * picked.shape[0], picked.shape[0], 0
         )

time: 504 us -> 482 us (0.956)
  waiting for transfers between devices: 446 us -> 418 us
  starting transfers between devices: 0.31 us -> 7.22 us
    all_gather x2 -> x0, waiting for transfers between devices: 51.4 us -> none  [shards(): gathered = lax.all_gather(picked, 'row', axis=0, tiled=True)]
    ppermute x0 -> x6, waiting for transfers between devices: none -> 23.7 us  [the longest x4 23.7 us: ring_gather(): lax.ppermute(going_up, axis, [(d, (d + 1) % ways) for d in range(ways)])]
    ppermute x0 -> x6, starting transfers between devices: none -> 7.18 us  [the longest x4 3.67 us: ring_gather(): lax.ppermute(going_up, axis, [(d, (d + 1) % ways) for d in range(ways)])]
  transfers between devices with their start and end apart: 4 -> 8, of which waited for: 4 -> 6; matrix products, arithmetic and copies ran while one was open for 0% -> 0% of each run, Pallas kernels for 0% -> 0%
where the time goes in v1:
time: 482 us; the launch traced here: 481 us
  waiting for transfers between devices  418 us (87%)
  matrix products  34.9 us (7%)
  between operations  13.5 us (3%)
  starting transfers between devices  7.22 us (1%)
    psum x2, waiting for transfers between devices, broadcast(): return lax.psum(jnp.where(mine, x, jnp.zeros_like(x)), axis)  394 us
    dot_general x4, matrix products, exact_dot(): jnp.dot(left_side, right_side, precision=lax.Precision.HIGHEST, preferred...  34.9 us
    ppermute x4, waiting for transfers between devices, ring_gather(): lax.ppermute(going_up, axis, [(d, (d + 1) % ways) for d in range(ways)])  23.7 us
  transfers between devices with their start and end apart: 8, of which 6 were waited for; matrix products, arithmetic and copies ran while one was open for 0% of the time, Pallas kernels for 0%

profile of v1, /device:TPU:2, one launch (start us, length us, event | category | flops | bytes accessed | tf_op | source)
XLA Modules:
  0.0 481.0 jit_solution(13205620879647082422)
XLA Ops:
  6.5 3.5 broadcast_select_fusion.9
  10.1 0.1 fusion.29
  10.2 199.4 %all-reduce.7.cloned.1.call-done = (f32[2048,128]{1,0:T(8,128)}, f32[2048,128]{1,0:T(8,128)}, f32[2048,128]{1,0:T(8,128)}, f32[2048,128]{1,0:T(8,128)}) async-done(((f32[2048,128]{1,0:T(8,128)}, f32[2048,128]{1,0:T(8,128)}, f32[2048,128]{1,0:T(8,128)}, f32[2048,128]{1,0:T(8,128)}), (f32[2048,128]{1,0:T(8,128)}, f32[2048,128]{1,0:T(8,128)}, f32[2048,128]{1,0:T(8,128)}, ...) | async-done | bytes 4194320 | tf_op jit(solution)/shard_map/psum | solution.py:25
  209.6 9.8 %broadcast_select_fusion = (f32[2048,512]{1,0:T(8,128)S(1)}, f32[2048,512]{1,0:T(8,128)}) fusion(pred[2048]{0:T(1024)(128)(4,1)S(1)} %get-tuple-element.39, f32[2,512,512]{2,1,0:T(8,128)S(1)} %copy-done.3, f32[2048,128]{1,0:T(8,128)} %get-tuple-element.21, f32[2048,128]{1,0:T(8,128)} %get-tuple-element.22, f32[2048,128]{1,0:T(8,128)} %get-tuple-element.23, ...), kind=kOutput, calls=%fused_computation.20 | convolution fusion | flops 6446645248 | bytes 13633536 | tf_op jit(solution)/shard_map/dot_general | solution.py:29
  219.4 0.1 broadcast.86.clone
  219.5 1.9 copy-done
  221.4 0.1 constant_dynamic-update-slice_fusion.7
  221.4 1.6 collective-permute-start
  223.0 1.8 collective-permute-start.1
  224.8 4.6 collective-permute-done
  229.4 0.3 collective-permute-start.2
  229.7 7.2 %collective-permute-done.2 = f32[128,512]{1,0:T(8,128)S(1)} collective-permute-done((f32[128,512]{1,0:T(8,128)S(1)}, f32[128,512]{1,0:T(8,128)S(1)}, u32[]{:S(2)}, u32[]{:S(2)}) %collective-permute-start.2) | collective-permute-done | bytes 262176 | tf_op jit(solution)/shard_map/ppermute | solution.py:13
  237.0 8.0 %broadcast_select_fusion.5 = (f32[2048,128]{1,0:T(8,128)}, f32[2048,128]{1,0:T(8,128)}, f32[2048,128]{1,0:T(8,128)}, f32[2048,128]{1,0:T(8,128)}, f32[2048,128]{1,0:T(8,128)S(1)}) fusion(pred[]{:T(512)S(6)} %eq.32, pred[]{:T(512)S(6)} %eq.39, pred[]{:T(512)S(6)} %eq.38, pred[]{:T(512)S(6)} %eq.37, f32[2048,128]{1,0:T(8,128)S(1)} %bitcast.38, ...), kind=kOutput, calls=%fused_computation.31 | convolution fusion | flops 1612447744 | bytes 11798541 | tf_op jit(solution)/shard_map/dot_general | solution.py:29
  245.0 194.4 %all-reduce.5.cloned.1.call-done = (f32[2048,128]{1,0:T(8,128)}, f32[2048,128]{1,0:T(8,128)}, f32[2048,128]{1,0:T(8,128)}, f32[2048,128]{1,0:T(8,128)}) async-done(((f32[2048,128]{1,0:T(8,128)}, f32[2048,128]{1,0:T(8,128)}, f32[2048,128]{1,0:T(8,128)}, f32[2048,128]{1,0:T(8,128)}), (f32[2048,128]{1,0:T(8,128)}, f32[2048,128]{1,0:T(8,128)}, f32[2048,128]{1,0:T(8,128)}, ...) | async-done | bytes 4194320 | tf_op jit(solution)/shard_map/psum | solution.py:25
  439.4 10.3 %broadcast_select_fusion.1 = (f32[2048,512]{1,0:T(8,128)S(1)}, f32[2048,512]{1,0:T(8,128)}) fusion(pred[2048]{0:T(1024)(128)(4,1)S(1)} %get-tuple-element.37, f32[2,512,512]{2,1,0:T(8,128)} %param.5, f32[2048,128]{1,0:T(8,128)} %get-tuple-element.17, f32[2048,128]{1,0:T(8,128)} %get-tuple-element.18, f32[2048,128]{1,0:T(8,128)} %get-tuple-element.19, ...), kind=kOutput, calls=%fused_computation.21 | convolution fusion | flops 6446645248 | bytes 13633536 | tf_op jit(solution)/shard_map/dot_general | solution.py:29
  449.6 0.1 broadcast.86
  449.8 1.9 copy-done.1
  451.6 0.1 constant_dynamic-update-slice_fusion.3
  451.7 1.6 collective-permute-start.3
  453.2 1.8 collective-permute-start.4
  455.0 4.6 collective-permute-done.3
  459.6 0.3 collective-permute-start.5
  459.9 7.2 %collective-permute-done.5 = f32[128,512]{1,0:T(8,128)S(1)} collective-permute-done((f32[128,512]{1,0:T(8,128)S(1)}, f32[128,512]{1,0:T(8,128)S(1)}, u32[]{:S(2)}, u32[]{:S(2)}) %collective-permute-start.5) | collective-permute-done | bytes 262176 | tf_op jit(solution)/shard_map/ppermute | solution.py:13
  467.2 6.9 %fusion.16 = f32[2048,128]{1,0:T(8,128)} fusion(f32[2048,128]{1,0:T(8,128)S(1)} %get-tuple-element.42, f32[2048,512]{1,0:T(8,128)} %copy-done.1, f32[2048,512]{1,0:T(8,128)} %get-tuple-element.44, s32[]{:T(128)S(6)} %select_n.178, pred[2048]{0:T(1024)(128)(4,1)S(1)} %get-tuple-element.39, pred[]{:T(512)S(6)} %and.36, ...), kind=kOutput, calls=%fused_computation.17 | convolution fusion | flops 1611399168 | bytes 7604233 | tf_op jit(solution)/shard_map/dot_general | solution.py:29
  (19 shorter events, 0.2 us)
Async XLA Ops:
  6.5 203.1 %all-reduce.7.cloned.1.call-start = ((), (), s32[]{:S(2)}) async-start(), calls=%async_computation.1 | async-start | bytes 8388608 | tf_op jit(solution)/shard_map/psum | solution.py:25
  6.5 203.1 %copy-start.3 = (f32[2,512,512]{2,1,0:T(8,128)S(1)}, f32[2,512,512]{2,1,0:T(8,128)}, u32[]{:S(2)}) copy-start(f32[2,512,512]{2,1,0:T(8,128)} %param.5) | copy-start | bytes 6291460
  10.0 429.3 %all-reduce.5.cloned.1.call-start = ((), (), s32[]{:S(2)}) async-start(), calls=%async_computation | async-start | bytes 8388608 | tf_op jit(solution)/shard_map/psum | solution.py:25
  219.4 2.0 copy-start
  219.4 17.6 %copy-start.2 = (f32[16,128,1,128]{3,2,1,0:T(1,128)S(1)}, f32[16,128,1,128]{3,2,1,0:T(1,128)}, u32[]{:S(2)}) copy-start(f32[16,128,1,128]{3,2,1,0:T(1,128)} %param.4) | copy-start | bytes 3145732
  221.4 7.9 %collective-permute-start = (f32[128,512]{1,0:T(8,128)S(1)}, f32[128,512]{1,0:T(8,128)S(1)}, u32[]{:S(2)}, u32[]{:S(2)}) collective-permute-start(f32[128,512]{1,0:T(8,128)S(1)} %get-tuple-element.28), channel_id=1, source_target_pairs={{0,1},{1,2},{2,3},{3,0},{4,5},{5,6},{6,7},{7,4},{8,9},{9,10},{10,1... | collective-permute-start | bytes 786440 | tf_op jit(solution)/shard_map/ppermute | solution.py:13
  223.0 6.7 %collective-permute-start.1 = (f32[128,512]{1,0:T(8,128)S(1)}, f32[128,512]{1,0:T(8,128)S(1)}, u32[]{:S(2)}, u32[]{:S(2)}) collective-permute-start(f32[128,512]{1,0:T(8,128)S(1)} %get-tuple-element.28), channel_id=1, source_target_pairs={{0,3},{1,0},{2,1},{3,2},{4,7},{5,4},{6,5},{7,6},{8,11},{9,8},{10,9... | collective-permute-start | bytes 786440 | tf_op jit(solution)/shard_map/ppermute | solution.py:16
  229.4 7.6 %collective-permute-start.2 = (f32[128,512]{1,0:T(8,128)S(1)}, f32[128,512]{1,0:T(8,128)S(1)}, u32[]{:S(2)}, u32[]{:S(2)}) collective-permute-start(f32[128,512]{1,0:T(8,128)S(1)} %collective-permute-done), channel_id=1, source_target_pairs={{0,1},{1,2},{2,3},{3,0},{4,5},{5,6},{6,7},{7,4},{8,9},{9,10},{10,1... | collective-permute-start | bytes 786440 | tf_op jit(solution)/shard_map/ppermute | solution.py:13
  449.6 2.0 copy-start.1
  451.7 7.9 %collective-permute-start.3 = (f32[128,512]{1,0:T(8,128)S(1)}, f32[128,512]{1,0:T(8,128)S(1)}, u32[]{:S(2)}, u32[]{:S(2)}) collective-permute-start(f32[128,512]{1,0:T(8,128)S(1)} %get-tuple-element.26), channel_id=1, source_target_pairs={{0,1},{1,2},{2,3},{3,0},{4,5},{5,6},{6,7},{7,4},{8,9},{9,10},{10,1... | collective-permute-start | bytes 786440 | tf_op jit(solution)/shard_map/ppermute | solution.py:13
  453.2 6.7 %collective-permute-start.4 = (f32[128,512]{1,0:T(8,128)S(1)}, f32[128,512]{1,0:T(8,128)S(1)}, u32[]{:S(2)}, u32[]{:S(2)}) collective-permute-start(f32[128,512]{1,0:T(8,128)S(1)} %get-tuple-element.26), channel_id=1, source_target_pairs={{0,3},{1,0},{2,1},{3,2},{4,7},{5,4},{6,5},{7,6},{8,11},{9,8},{10,9... | collective-permute-start | bytes 786440 | tf_op jit(solution)/shard_map/ppermute | solution.py:16
  459.6 7.6 %collective-permute-start.5 = (f32[128,512]{1,0:T(8,128)S(1)}, f32[128,512]{1,0:T(8,128)S(1)}, u32[]{:S(2)}, u32[]{:S(2)}) collective-permute-start(f32[128,512]{1,0:T(8,128)S(1)} %collective-permute-done.3), channel_id=1, source_target_pairs={{0,1},{1,2},{2,3},{3,0},{4,5},{5,6},{6,7},{7,4},{8,9},{9,10},{10,1... | collective-permute-start | bytes 786440 | tf_op jit(solution)/shard_map/ppermute | solution.py:13
Sparse Core Ops, SparseCore 0:
  11.3 198.2 all-reduce.6
  245.1 194.2 all-reduce.4
